TPU v7x, 128 devices: a whole 4x4x4 slice. The times are simulated.
128 devices in a mesh: row: 8 (over z, core), col: 16 (over y, x).
Axes of the slice: x: 4, y: 4, z: 4, core: 2. Of those that a mesh axis runs over, the one named last changes fastest.
Arguments:
- hidden: bfloat16 [1408, 16384], P('col', 'row'), may hold values from -18 to 18
- gain_in: bfloat16 [1408], replicated, may hold values from 0.5 to 1.5
- w_query: bfloat16 [1408, 1408], P('col'), may hold values from -0.3125 to 0.3125
- w_pair: bfloat16 [2, 1408, 1408], P(None, 'col'), may hold values from -0.15625 to 0.15625
- kv_cache: bfloat16 [2, 1408, 16384], P(None, 'col', 'row'), may hold values from -103 to 103
- recompute_rows: int32 [8, 200], P('row'), may hold values from 0 to 2047, as said below
- segment_ids: int32 [16384], P('row'), may hold values from -1 to 1, as said below
- w_out: bfloat16 [1408, 1408], P('col'), may hold values from -0.3125 to 0.3125
- gain_merge: bfloat16 [1408], replicated, may hold values from 0.5 to 1.5
- w_merge: bfloat16 [4, 1408, 1408], P(None, 'col'), may hold values from -0.078125 to 0.078125
- requests: int32 [8, 16, 85], P('row'), may hold values from -1 to 511, as said below
Outputs:
- delivered: bfloat16 [8, 16, 85, 1408], P('row', 'col')
Inputs may be any that keep to these rules, and one draw needn't show every extreme that they name: `segment_ids`: ids do not fall along the tokens except to -1 for the padding at the end; every image covers a multiple of 4 tokens and starts at a multiple of 4. `recompute_rows`: the 200 offsets of one index of row are distinct. `requests`: for each index of row, the lists of all owners together name each of its 512 merged tokens exactly once; unused slots hold -1 and follow the used ones.
All inputs are finite; a program needn't handle non-finite values.
Results may differ from a plain program's by a relative error of at most 0.025.
The roundings to bfloat16 on the way count: a program that leaves them out, or rounds other values in their place, can miss the bound.
Values may be sent and summed in bfloat16 or wider, within the bound.
A program may use at most 128 MiB of HBM per device.

v0:
```python
import jax
import jax.numpy as jnp
from jax import lax
from jax.sharding import PartitionSpec as P

HD = 88
EPSILON = 1e-06
MASKED = -1e30
KEY_BLOCK = 1024


def on_device(
    hidden,
    gain_in,
    w_query,
    w_pair,
    kv_cache,
    recompute_rows,
    segment_ids,
    w_out,
    gain_merge,
    w_merge,
    requests,
):
    local_width, tok_rows = hidden.shape
    model_width = w_query.shape[1]
    n_col = model_width // local_width
    heads_here = local_width // HD
    score_scale = HD ** (-0.5)
    col_index = lax.axis_index("col")
    full_rows = lax.all_gather(hidden, "col", axis=0, tiled=True)
    out_weight = lax.all_gather(w_out, "col", axis=0, tiled=True)
    full_float = full_rows.astype(jnp.float32)
    in_mean = jnp.sum(full_float, axis=0, keepdims=True) / model_width
    in_square = jnp.sum(full_float * full_float, axis=0, keepdims=True) / model_width
    normed = (
        (full_float - in_mean)
        * lax.rsqrt(in_square - in_mean * in_mean + EPSILON)
        * gain_in.astype(jnp.float32)[:, None]
    ).astype(jnp.bfloat16)
    queries = jnp.dot(w_query, normed, preferred_element_type=jnp.float32).astype(jnp.bfloat16)
    picked_rows = recompute_rows[0]
    normed_picked = jnp.take(normed, picked_rows, axis=1)
    fresh_pairs = jnp.dot(
        w_pair.reshape(2 * local_width, model_width),
        normed_picked,
        preferred_element_type=jnp.float32,
    )
    fresh_pairs = fresh_pairs.astype(jnp.bfloat16).reshape(2, local_width, -1)
    keys_values = kv_cache.at[:, :, picked_rows].set(fresh_pairs)
    query_heads = queries.reshape(heads_here, HD, tok_rows)
    pair_local = jnp.concatenate(
        [keys_values.reshape(2 * local_width, tok_rows), segment_ids.astype(jnp.bfloat16)[None, :]],
        axis=0,
    )
    pair_all = lax.all_gather(pair_local, "row", axis=1, tiled=True)
    pair_rows = pair_all[: 2 * local_width].reshape(2, local_width, -1)
    segment_line = pair_all[2 * local_width].astype(jnp.int32)

    def take_block(carried, pair_block, segment_block):
        running_max, running_sum, weighted = carried
        key_block = pair_block[0].reshape(heads_here, HD, -1)
        value_block = pair_block[1].reshape(heads_here, HD, -1)
        scores = (
            jnp.einsum("hdq,hdk->hqk", query_heads, key_block, preferred_element_type=jnp.float32)
            * score_scale
        )
        allowed = (segment_ids[:, None] == segment_block[None, :])[None, :, :]
        new_max = jnp.maximum(running_max, jnp.max(jnp.where(allowed, scores, MASKED), axis=2))
        weights_exp = jnp.where(allowed, jnp.exp(scores - new_max[:, :, None]), 0.0)
        factor = jnp.exp(running_max - new_max)
        running_sum = running_sum * factor + jnp.sum(weights_exp, axis=2)
        product = jnp.einsum(
            "hqk,hdk->hdq",
            weights_exp.astype(jnp.bfloat16),
            value_block,
            preferred_element_type=jnp.float32,
        )
        weighted = weighted * factor[:, None, :] + product
        return (new_max, running_sum, weighted)

    starting = (
        jnp.full((heads_here, tok_rows), MASKED, jnp.float32),
        jnp.zeros((heads_here, tok_rows), jnp.float32),
        jnp.zeros((heads_here, HD, tok_rows), jnp.float32),
    )
    piece_rows = pair_rows.shape[2]
    whole_blocks = piece_rows // KEY_BLOCK

    def loop_body(block_index, loop_state):
        pair_block = lax.dynamic_slice_in_dim(pair_rows, block_index * KEY_BLOCK, KEY_BLOCK, 2)
        segment_block = lax.dynamic_slice_in_dim(
            segment_line, block_index * KEY_BLOCK, KEY_BLOCK, 0
        )
        return take_block(loop_state, pair_block, segment_block)

    running_max, running_sum, weighted = lax.fori_loop(0, whole_blocks, loop_body, starting)
    attended = (
        (weighted / running_sum[:, None, :]).astype(jnp.bfloat16).reshape(local_width, tok_rows)
    )
    chunk = tok_rows // n_col
    attended_chunk = lax.all_to_all(attended, "col", 1, 0, tiled=True)
    x_chunk = lax.dynamic_slice_in_dim(full_float, col_index * chunk, chunk, 1)
    projected = lax.dot_general(
        out_weight, attended_chunk, (((0,), (0,)), ((), ())), preferred_element_type=jnp.float32
    )
    updated = x_chunk + projected
    row_mean = jnp.sum(updated, axis=0, keepdims=True) / model_width
    row_square = jnp.sum(updated * updated, axis=0, keepdims=True) / model_width
    merger_chunk = (
        (updated - row_mean)
        * lax.rsqrt(row_square - row_mean * row_mean + EPSILON)
        * gain_merge.astype(jnp.float32)[:, None]
    ).astype(jnp.bfloat16)
    merger_in = lax.all_to_all(merger_chunk, "col", 0, 1, tiled=True)
    merged_rows = tok_rows // 4
    grouped = merger_in.reshape(local_width, merged_rows, 4)
    merged = jnp.einsum("cgi,icd->gd", grouped, w_merge, preferred_element_type=jnp.float32)
    merged_sum = lax.psum(merged.astype(jnp.bfloat16), "col")
    wanted_rows = lax.dynamic_index_in_dim(requests[0], col_index, 0, keepdims=False)
    is_valid = wanted_rows >= 0
    safe_index = jnp.where(is_valid, wanted_rows, 0)
    picked = jnp.where(is_valid[:, None], merged_sum[safe_index], jnp.zeros((), jnp.bfloat16))
    return picked.reshape(1, 1, picked.shape[0], model_width)


def solution(mesh):
    placed = (
        P("col", "row"),
        P(),
        P("col", None),
        P(None, "col", None),
        P(None, "col", "row"),
        P("row", None),
        P("row"),
        P("col", None),
        P(),
        P(None, "col", None),
        P("row", None, None),
    )
    return jax.shard_map(
        on_device,
        mesh=mesh,
        in_specs=placed,
        out_specs=P("row", "col", None, None),
        check_vma=False,
    )
```

profile of v0, /device:TPU:0, one launch (start us, length us, event | category | flops | bytes accessed | tf_op | source)
XLA Modules:
  0.0 532.2 jit_solution(17478060739190972676)
XLA Ops:
  12.5 58.2 %all-gather.4.cloned.1.call-done = bf16[1408,2048]{1,0:T(8,128)(2,1)} async-done(((bf16[88,2048]{1,0:T(8,128)(2,1)}), bf16[1408,2048]{1,0:T(8,128)(2,1)}) %all-gather.4.cloned.1.call-update) | async-done | bytes 5767184 | tf_op jit(solution)/shard_map/all_gather | solution.py:31
  70.7 8.3 %copy.31 = bf16[1408,2048]{0,1:T(8,128)(2,1)} copy(bf16[1408,2048]{1,0:T(8,128)(2,1)} %all-gather.4.cloned.1.call-done) | data formatting | bytes 11534336 | tf_op jit(solution)/shard_map/all_gather | solution.py:31
  93.1 6.9 %scatter_fusion = bf16[2,88,2048]{1,0,2:T(2,128)(2,1)S(1)} fusion(bf16[2,88,2048]{1,0,2:T(2,128)(2,1)S(1)} %copy.33, s32[200]{0:T(256)S(1)} %bitcast.125, bf16[200,2,88]{2,1,0:T(2,128)(2,1)S(1)} %bitcast.118), kind=kCustom, calls=%fused_computation.2 | custom fusion | bytes 212000 | tf_op jit(solution)/shard_map/scatter | solution.py:50
  107.2 34.4 %all-gather.6.cloned.1.call-done = bf16[177,16384]{1,0:T(8,128)(2,1)} async-done(((bf16[177,2048]{1,0:T(8,128)(2,1)}), bf16[177,16384]{1,0:T(8,128)(2,1)}) %all-gather.6.cloned.1.call-update) | async-done | bytes 5799952 | tf_op jit(solution)/shard_map/all_gather | solution.py:56
  141.7 5.8 %slice.29 = bf16[176,16384]{1,0:T(8,128)(2,1)} slice(bf16[177,16384]{1,0:T(8,128)(2,1)} %all-gather.6.cloned.1.call-done), slice={[0:176], [0:16384]} | slice | bytes 11534336 | tf_op jit(solution)/shard_map/slice | solution.py:57
  148.4 251.7 %while.18 = (s32[]{:T(128)}, f32[1,2048]{1,0:T(1,128)S(1)}, f32[1,2048]{1,0:T(1,128)S(1)}, f32[1,88,2048]{2,1,0:T(8,128)S(1)}, s32[2048]{0:T(1024)S(1)}, /*index...) while((s32[]{:T(128)}, f32[1,2048]{1,0:T(1,128)S(1)}, ...), condition=%wide.region_6.7_spmd.clone, body=%wide.region_3.0_spmd.clone.sunk | while | flops 768108544 | bytes 27504848 | solution.py:97
  148.5 5.6 %fusion.45 = (f32[2048]{0:T(1024)S(1)}, f32[1024,2048]{1,0:T(8,128)}) fusion(s32[2048]{0:T(1024)S(1)} %get-tuple-element.290, s32[1024]{0:T(1024)S(1)} %dynamic_slice.32, bf16[1,88,2048]{2,1,0:T(8,128)(2,1)S(1)} %get-tuple-element.293, bf16[2,88,16384]{2,1,0:T(8,128)(2,1)} %get-tuple-element.292, s32[]{:T(128)S(6)} %select_n.132), kind=kOutput, calls=%fused_computation.5.clone.1 | convolution fusion | flops 377485312 | bytes 8949764 | tf_op jit(solution)/shard_map/while/body/eval_jaxpr/hdq,hdk->hqk/dot_general | solution.py:65
  158.8 5.5 %fusion.49 = f32[1,88,2048]{2,1,0:T(8,128)S(1)} fusion(f32[1024,2048]{1,0:T(8,128)} %get-tuple-element.257, f32[2048]{0:T(1024)S(1)} %bitcast.110, s32[2048]{0:T(1024)S(1)} %get-tuple-element.290, s32[1024]{0:T(1024)S(1)} %dynamic_slice.32, f32[1,88,2048]{2,1,0:T(8,128)S(1)} %get-tuple-element.276, f32[2048]{0:T(1024)S(1)} %bitcast.120, ...), kind=kOutput, calls=%fused_computation.12.clone.1 | convolution fusion | flops 380125184 | bytes 10039305 | tf_op jit(solution)/shard_map/while/body/eval_jaxpr/hqk,hdk->hdq/dot_general | solution.py:73
  164.3 5.6 %fusion.45 = (f32[2048]{0:T(1024)S(1)}, f32[1024,2048]{1,0:T(8,128)}) fusion(s32[2048]{0:T(1024)S(1)} %get-tuple-element.290, s32[1024]{0:T(1024)S(1)} %dynamic_slice.32, bf16[1,88,2048]{2,1,0:T(8,128)(2,1)S(1)} %get-tuple-element.293, bf16[2,88,16384]{2,1,0:T(8,128)(2,1)} %get-tuple-element.292, s32[]{:T(128)S(6)} %select_n.132), kind=kOutput, calls=%fused_computation.5.clone.1 | convolution fusion | flops 377485312 | bytes 8949764 | tf_op jit(solution)/shard_map/while/body/eval_jaxpr/hdq,hdk->hqk/dot_general | solution.py:65
  174.5 5.4 %fusion.49 = f32[1,88,2048]{2,1,0:T(8,128)S(1)} fusion(f32[1024,2048]{1,0:T(8,128)} %get-tuple-element.257, f32[2048]{0:T(1024)S(1)} %bitcast.110, s32[2048]{0:T(1024)S(1)} %get-tuple-element.290, s32[1024]{0:T(1024)S(1)} %dynamic_slice.32, f32[1,88,2048]{2,1,0:T(8,128)S(1)} %get-tuple-element.276, f32[2048]{0:T(1024)S(1)} %bitcast.120, ...), kind=kOutput, calls=%fused_computation.12.clone.1 | convolution fusion | flops 380125184 | bytes 10039305 | tf_op jit(solution)/shard_map/while/body/eval_jaxpr/hqk,hdk->hdq/dot_general | solution.py:73
  180.0 5.6 %fusion.45 = (f32[2048]{0:T(1024)S(1)}, f32[1024,2048]{1,0:T(8,128)}) fusion(s32[2048]{0:T(1024)S(1)} %get-tuple-element.290, s32[1024]{0:T(1024)S(1)} %dynamic_slice.32, bf16[1,88,2048]{2,1,0:T(8,128)(2,1)S(1)} %get-tuple-element.293, bf16[2,88,16384]{2,1,0:T(8,128)(2,1)} %get-tuple-element.292, s32[]{:T(128)S(6)} %select_n.132), kind=kOutput, calls=%fused_computation.5.clone.1 | convolution fusion | flops 377485312 | bytes 8949764 | tf_op jit(solution)/shard_map/while/body/eval_jaxpr/hdq,hdk->hqk/dot_general | solution.py:65
  195.9 5.6 %fusion.45 = (f32[2048]{0:T(1024)S(1)}, f32[1024,2048]{1,0:T(8,128)}) fusion(s32[2048]{0:T(1024)S(1)} %get-tuple-element.290, s32[1024]{0:T(1024)S(1)} %dynamic_slice.32, bf16[1,88,2048]{2,1,0:T(8,128)(2,1)S(1)} %get-tuple-element.293, bf16[2,88,16384]{2,1,0:T(8,128)(2,1)} %get-tuple-element.292, s32[]{:T(128)S(6)} %select_n.132), kind=kOutput, calls=%fused_computation.5.clone.1 | convolution fusion | flops 377485312 | bytes 8949764 | tf_op jit(solution)/shard_map/while/body/eval_jaxpr/hdq,hdk->hqk/dot_general | solution.py:65
  211.6 5.6 %fusion.45 = (f32[2048]{0:T(1024)S(1)}, f32[1024,2048]{1,0:T(8,128)}) fusion(s32[2048]{0:T(1024)S(1)} %get-tuple-element.290, s32[1024]{0:T(1024)S(1)} %dynamic_slice.32, bf16[1,88,2048]{2,1,0:T(8,128)(2,1)S(1)} %get-tuple-element.293, bf16[2,88,16384]{2,1,0:T(8,128)(2,1)} %get-tuple-element.292, s32[]{:T(128)S(6)} %select_n.132), kind=kOutput, calls=%fused_computation.5.clone.1 | convolution fusion | flops 377485312 | bytes 8949764 | tf_op jit(solution)/shard_map/while/body/eval_jaxpr/hdq,hdk->hqk/dot_general | solution.py:65
  227.3 5.6 %fusion.45 = (f32[2048]{0:T(1024)S(1)}, f32[1024,2048]{1,0:T(8,128)}) fusion(s32[2048]{0:T(1024)S(1)} %get-tuple-element.290, s32[1024]{0:T(1024)S(1)} %dynamic_slice.32, bf16[1,88,2048]{2,1,0:T(8,128)(2,1)S(1)} %get-tuple-element.293, bf16[2,88,16384]{2,1,0:T(8,128)(2,1)} %get-tuple-element.292, s32[]{:T(128)S(6)} %select_n.132), kind=kOutput, calls=%fused_computation.5.clone.1 | convolution fusion | flops 377485312 | bytes 8949764 | tf_op jit(solution)/shard_map/while/body/eval_jaxpr/hdq,hdk->hqk/dot_general | solution.py:65
  237.6 5.4 %fusion.49 = f32[1,88,2048]{2,1,0:T(8,128)S(1)} fusion(f32[1024,2048]{1,0:T(8,128)} %get-tuple-element.257, f32[2048]{0:T(1024)S(1)} %bitcast.110, s32[2048]{0:T(1024)S(1)} %get-tuple-element.290, s32[1024]{0:T(1024)S(1)} %dynamic_slice.32, f32[1,88,2048]{2,1,0:T(8,128)S(1)} %get-tuple-element.276, f32[2048]{0:T(1024)S(1)} %bitcast.120, ...), kind=kOutput, calls=%fused_computation.12.clone.1 | convolution fusion | flops 380125184 | bytes 10039305 | tf_op jit(solution)/shard_map/while/body/eval_jaxpr/hqk,hdk->hdq/dot_general | solution.py:73
  243.0 5.6 %fusion.45 = (f32[2048]{0:T(1024)S(1)}, f32[1024,2048]{1,0:T(8,128)}) fusion(s32[2048]{0:T(1024)S(1)} %get-tuple-element.290, s32[1024]{0:T(1024)S(1)} %dynamic_slice.32, bf16[1,88,2048]{2,1,0:T(8,128)(2,1)S(1)} %get-tuple-element.293, bf16[2,88,16384]{2,1,0:T(8,128)(2,1)} %get-tuple-element.292, s32[]{:T(128)S(6)} %select_n.132), kind=kOutput, calls=%fused_computation.5.clone.1 | convolution fusion | flops 377485312 | bytes 8949764 | tf_op jit(solution)/shard_map/while/body/eval_jaxpr/hdq,hdk->hqk/dot_general | solution.py:65
  253.3 5.4 %fusion.49 = f32[1,88,2048]{2,1,0:T(8,128)S(1)} fusion(f32[1024,2048]{1,0:T(8,128)} %get-tuple-element.257, f32[2048]{0:T(1024)S(1)} %bitcast.110, s32[2048]{0:T(1024)S(1)} %get-tuple-element.290, s32[1024]{0:T(1024)S(1)} %dynamic_slice.32, f32[1,88,2048]{2,1,0:T(8,128)S(1)} %get-tuple-element.276, f32[2048]{0:T(1024)S(1)} %bitcast.120, ...), kind=kOutput, calls=%fused_computation.12.clone.1 | convolution fusion | flops 380125184 | bytes 10039305 | tf_op jit(solution)/shard_map/while/body/eval_jaxpr/hqk,hdk->hdq/dot_general | solution.py:73
  258.7 5.6 %fusion.45 = (f32[2048]{0:T(1024)S(1)}, f32[1024,2048]{1,0:T(8,128)}) fusion(s32[2048]{0:T(1024)S(1)} %get-tuple-element.290, s32[1024]{0:T(1024)S(1)} %dynamic_slice.32, bf16[1,88,2048]{2,1,0:T(8,128)(2,1)S(1)} %get-tuple-element.293, bf16[2,88,16384]{2,1,0:T(8,128)(2,1)} %get-tuple-element.292, s32[]{:T(128)S(6)} %select_n.132), kind=kOutput, calls=%fused_computation.5.clone.1 | convolution fusion | flops 377485312 | bytes 8949764 | tf_op jit(solution)/shard_map/while/body/eval_jaxpr/hdq,hdk->hqk/dot_general | solution.py:65
  274.4 5.6 %fusion.45 = (f32[2048]{0:T(1024)S(1)}, f32[1024,2048]{1,0:T(8,128)}) fusion(s32[2048]{0:T(1024)S(1)} %get-tuple-element.290, s32[1024]{0:T(1024)S(1)} %dynamic_slice.32, bf16[1,88,2048]{2,1,0:T(8,128)(2,1)S(1)} %get-tuple-element.293, bf16[2,88,16384]{2,1,0:T(8,128)(2,1)} %get-tuple-element.292, s32[]{:T(128)S(6)} %select_n.132), kind=kOutput, calls=%fused_computation.5.clone.1 | convolution fusion | flops 377485312 | bytes 8949764 | tf_op jit(solution)/shard_map/while/body/eval_jaxpr/hdq,hdk->hqk/dot_general | solution.py:65
  290.2 5.6 %fusion.45 = (f32[2048]{0:T(1024)S(1)}, f32[1024,2048]{1,0:T(8,128)}) fusion(s32[2048]{0:T(1024)S(1)} %get-tuple-element.290, s32[1024]{0:T(1024)S(1)} %dynamic_slice.32, bf16[1,88,2048]{2,1,0:T(8,128)(2,1)S(1)} %get-tuple-element.293, bf16[2,88,16384]{2,1,0:T(8,128)(2,1)} %get-tuple-element.292, s32[]{:T(128)S(6)} %select_n.132), kind=kOutput, calls=%fused_computation.5.clone.1 | convolution fusion | flops 377485312 | bytes 8949764 | tf_op jit(solution)/shard_map/while/body/eval_jaxpr/hdq,hdk->hqk/dot_general | solution.py:65
  305.9 5.6 %fusion.45 = (f32[2048]{0:T(1024)S(1)}, f32[1024,2048]{1,0:T(8,128)}) fusion(s32[2048]{0:T(1024)S(1)} %get-tuple-element.290, s32[1024]{0:T(1024)S(1)} %dynamic_slice.32, bf16[1,88,2048]{2,1,0:T(8,128)(2,1)S(1)} %get-tuple-element.293, bf16[2,88,16384]{2,1,0:T(8,128)(2,1)} %get-tuple-element.292, s32[]{:T(128)S(6)} %select_n.132), kind=kOutput, calls=%fused_computation.5.clone.1 | convolution fusion | flops 377485312 | bytes 8949764 | tf_op jit(solution)/shard_map/while/body/eval_jaxpr/hdq,hdk->hqk/dot_general | solution.py:65
  316.1 5.4 %fusion.49 = f32[1,88,2048]{2,1,0:T(8,128)S(1)} fusion(f32[1024,2048]{1,0:T(8,128)} %get-tuple-element.257, f32[2048]{0:T(1024)S(1)} %bitcast.110, s32[2048]{0:T(1024)S(1)} %get-tuple-element.290, s32[1024]{0:T(1024)S(1)} %dynamic_slice.32, f32[1,88,2048]{2,1,0:T(8,128)S(1)} %get-tuple-element.276, f32[2048]{0:T(1024)S(1)} %bitcast.120, ...), kind=kOutput, calls=%fused_computation.12.clone.1 | convolution fusion | flops 380125184 | bytes 10039305 | tf_op jit(solution)/shard_map/while/body/eval_jaxpr/hqk,hdk->hdq/dot_general | solution.py:73
  321.6 5.6 %fusion.45 = (f32[2048]{0:T(1024)S(1)}, f32[1024,2048]{1,0:T(8,128)}) fusion(s32[2048]{0:T(1024)S(1)} %get-tuple-element.290, s32[1024]{0:T(1024)S(1)} %dynamic_slice.32, bf16[1,88,2048]{2,1,0:T(8,128)(2,1)S(1)} %get-tuple-element.293, bf16[2,88,16384]{2,1,0:T(8,128)(2,1)} %get-tuple-element.292, s32[]{:T(128)S(6)} %select_n.132), kind=kOutput, calls=%fused_computation.5.clone.1 | convolution fusion | flops 377485312 | bytes 8949764 | tf_op jit(solution)/shard_map/while/body/eval_jaxpr/hdq,hdk->hqk/dot_general | solution.py:65
  331.8 5.4 %fusion.49 = f32[1,88,2048]{2,1,0:T(8,128)S(1)} fusion(f32[1024,2048]{1,0:T(8,128)} %get-tuple-element.257, f32[2048]{0:T(1024)S(1)} %bitcast.110, s32[2048]{0:T(1024)S(1)} %get-tuple-element.290, s32[1024]{0:T(1024)S(1)} %dynamic_slice.32, f32[1,88,2048]{2,1,0:T(8,128)S(1)} %get-tuple-element.276, f32[2048]{0:T(1024)S(1)} %bitcast.120, ...), kind=kOutput, calls=%fused_computation.12.clone.1 | convolution fusion | flops 380125184 | bytes 10039305 | tf_op jit(solution)/shard_map/while/body/eval_jaxpr/hqk,hdk->hdq/dot_general | solution.py:73
  337.3 5.6 %fusion.45 = (f32[2048]{0:T(1024)S(1)}, f32[1024,2048]{1,0:T(8,128)}) fusion(s32[2048]{0:T(1024)S(1)} %get-tuple-element.290, s32[1024]{0:T(1024)S(1)} %dynamic_slice.32, bf16[1,88,2048]{2,1,0:T(8,128)(2,1)S(1)} %get-tuple-element.293, bf16[2,88,16384]{2,1,0:T(8,128)(2,1)} %get-tuple-element.292, s32[]{:T(128)S(6)} %select_n.132), kind=kOutput, calls=%fused_computation.5.clone.1 | convolution fusion | flops 377485312 | bytes 8949764 | tf_op jit(solution)/shard_map/while/body/eval_jaxpr/hdq,hdk->hqk/dot_general | solution.py:65
  353.0 5.6 %fusion.45 = (f32[2048]{0:T(1024)S(1)}, f32[1024,2048]{1,0:T(8,128)}) fusion(s32[2048]{0:T(1024)S(1)} %get-tuple-element.290, s32[1024]{0:T(1024)S(1)} %dynamic_slice.32, bf16[1,88,2048]{2,1,0:T(8,128)(2,1)S(1)} %get-tuple-element.293, bf16[2,88,16384]{2,1,0:T(8,128)(2,1)} %get-tuple-element.292, s32[]{:T(128)S(6)} %select_n.132), kind=kOutput, calls=%fused_computation.5.clone.1 | convolution fusion | flops 377485312 | bytes 8949764 | tf_op jit(solution)/shard_map/while/body/eval_jaxpr/hdq,hdk->hqk/dot_general | solution.py:65
  368.7 5.6 %fusion.45 = (f32[2048]{0:T(1024)S(1)}, f32[1024,2048]{1,0:T(8,128)}) fusion(s32[2048]{0:T(1024)S(1)} %get-tuple-element.290, s32[1024]{0:T(1024)S(1)} %dynamic_slice.32, bf16[1,88,2048]{2,1,0:T(8,128)(2,1)S(1)} %get-tuple-element.293, bf16[2,88,16384]{2,1,0:T(8,128)(2,1)} %get-tuple-element.292, s32[]{:T(128)S(6)} %select_n.132), kind=kOutput, calls=%fused_computation.5.clone.1 | convolution fusion | flops 377485312 | bytes 8949764 | tf_op jit(solution)/shard_map/while/body/eval_jaxpr/hdq,hdk->hqk/dot_general | solution.py:65
  384.4 5.6 %fusion.45 = (f32[2048]{0:T(1024)S(1)}, f32[1024,2048]{1,0:T(8,128)}) fusion(s32[2048]{0:T(1024)S(1)} %get-tuple-element.290, s32[1024]{0:T(1024)S(1)} %dynamic_slice.32, bf16[1,88,2048]{2,1,0:T(8,128)(2,1)S(1)} %get-tuple-element.293, bf16[2,88,16384]{2,1,0:T(8,128)(2,1)} %get-tuple-element.292, s32[]{:T(128)S(6)} %select_n.132), kind=kOutput, calls=%fused_computation.5.clone.1 | convolution fusion | flops 377485312 | bytes 8949764 | tf_op jit(solution)/shard_map/while/body/eval_jaxpr/hdq,hdk->hqk/dot_general | solution.py:65
  401.1 6.9 %all-to-all-start = ((bf16[88,16,128]{2,0,1:T(8,128)(2,1)}), bf16[88,16,128]{2,0,1:T(8,128)(2,1)S(1)}, u32[]{:S(2)}, u32[]{:S(2)}) async-start(bf16[88,16,128]{2,0,1:T(8,128)(2,1)} %copy.35), calls=%async_computation | async-start | bytes 720896 | tf_op jit(solution)/shard_map/all_to_all | solution.py:102
  408.1 7.6 %convert_element_type.50 = f32[1408,2048]{0,1:T(8,128)} convert(bf16[1408,2048]{0,1:T(8,128)(2,1)} %copy.31) | non-fusion elementwise | flops 2883584 | bytes 17301504 | tf_op jit(solution)/shard_map/convert_element_type | solution.py:33
  421.7 14.1 %all_to_all.35 = bf16[16,88,128]{2,1,0:T(8,128)(2,1)S(1)} all-to-all(bf16[16,88,128]{2,1,0:T(8,128)(2,1)S(1)} %bitcast.114), channel_id=1, replica_groups=mesh['row'=8,'col'=16] {'col'}, dimensions={0} | all-to-all | bytes 720896 | tf_op jit(solution)/shard_map/all_to_all | solution.py:115
  439.6 82.8 %all-reduce.2.cloned.1.call-done = bf16[512,1408]{1,0:T(8,128)(2,1)} async-done(((bf16[512,1408]{1,0:T(8,128)(2,1)}), bf16[512,1408]{1,0:T(8,128)(2,1)}) %all-reduce.2.cloned.1.call-update) | async-done | bytes 1441808 | tf_op jit(solution)/shard_map/psum | solution.py:119
  (147 shorter events, 170.8 us)
Async XLA Ops:
  6.5 429.6 %copy-start = (bf16[4,88,1408]{2,1,0:T(8,128)(2,1)S(1)}, bf16[4,88,1408]{2,1,0:T(8,128)(2,1)}, u32[]{:S(2)}) copy-start(bf16[4,88,1408]{2,1,0:T(8,128)(2,1)} %param.22) | copy-start | bytes 2973700
  6.5 64.2 %all-gather.4.cloned.1.call-start = ((), (), s32[]{:S(2)}) async-start(), calls=%async_computation.2 | async-start | bytes 6127616 | tf_op jit(solution)/shard_map/all_gather | solution.py:31
  7.3 134.4 %all-gather.6.cloned.1.call-start = ((), (), s32[]{:S(2)}) async-start(), calls=%async_computation.3 | async-start | bytes 6782976 | tf_op jit(solution)/shard_map/all_gather | solution.py:56
  79.1 4.5 copy-start.1
  83.6 9.0 %copy-start.5 = (bf16[2,88,1408]{2,1,0:T(8,128)(2,1)S(1)}, bf16[2,88,1408]{2,1,0:T(8,128)(2,1)}, u32[]{:S(2)}) copy-start(bf16[2,88,1408]{2,1,0:T(8,128)(2,1)} %param.16) | copy-start | bytes 1486852
  87.5 15.0 %copy-start.3 = (bf16[88,1408]{1,0:T(8,128)(2,1)S(1)}, bf16[88,1408]{1,0:T(8,128)(2,1)}, u32[]{:S(2)}) copy-start(bf16[88,1408]{1,0:T(8,128)(2,1)} %param.15) | copy-start | bytes 743428
  101.8 313.8 %all-gather.8.cloned.1.call-start = ((), (), s32[]{:S(2)}) async-start(), calls=%async_computation.4 | async-start | bytes 4212736 | tf_op jit(solution)/shard_map/all_gather | solution.py:32
  102.5 45.9 %copy-start.2 = (s32[2048]{0:T(1024)S(1)}, s32[2048]{0:T(1024)}, u32[]{:S(2)}) copy-start(s32[2048]{0:T(1024)} %param.19) | copy-start | bytes 24580
  148.4 259.6 %copy-start.4 = (bf16[1408]{0:T(1024)(128)(2,1)S(1)}, bf16[1408]{0:T(1024)(128)(2,1)}, u32[]{:S(2)}) copy-start(bf16[1408]{0:T(1024)(128)(2,1)} %param.21) | copy-start | bytes 8452
  401.1 17.0 %all-to-all-start = ((bf16[88,16,128]{2,0,1:T(8,128)(2,1)}), bf16[88,16,128]{2,0,1:T(8,128)(2,1)S(1)}, u32[]{:S(2)}, u32[]{:S(2)}) async-start(bf16[88,16,128]{2,0,1:T(8,128)(2,1)} %copy.35), calls=%async_computation | async-start | bytes 720896 | tf_op jit(solution)/shard_map/all_to_all | solution.py:102
  408.0 114.4 %all-reduce.2.cloned.1.call-start = ((), (), s32[]{:S(2)}) async-start(), calls=%async_computation.5 | async-start | bytes 2883584 | tf_op jit(solution)/shard_map/psum | solution.py:119
Sparse Core Ops, SparseCore 0:
  9.5 61.1 all-gather.3
  101.9 39.7 all-gather.5
  143.8 50.4 all-gather.7
  438.4 83.9 all-reduce.1
where the time goes:
time: 534 us; the launch traced here: 532 us
  matrix products  187 us (35%)
  waiting for transfers between devices  179 us (34%)
  other arithmetic  97.5 us (18%)
  local copies, waits for them, and re-layouts  33.4 us (6%)
  blocking collectives  14.1 us (3%)
  between operations  13.4 us (3%)
  starting transfers between devices  7.17 us (1%)
    dot_general x16, matrix products, take_block(): jnp.einsum('hdq,hdk->hqk', query_heads, key_block, preferred_element_type...  89.9 us
    dot_general x16, matrix products, take_block(): jnp.einsum('hqk,hdk->hdq', weights_exp.astype(jnp.bfloat16), value_block,...  86.4 us
    psum x1, waiting for transfers between devices, on_device(): merged_sum = lax.psum(merged.astype(jnp.bfloat16), 'col')  82.8 us
    reduce_sum x16, other arithmetic, take_block(): running_sum = running_sum * factor + jnp.sum(weights_exp, axis=2)  73.4 us
    all_gather x1, waiting for transfers between devices, on_device(): full_rows = lax.all_gather(hidden, 'col', axis=0, tiled=True)  58.2 us
    all_gather x1, waiting for transfers between devices, on_device(): pair_all = lax.all_gather(pair_local, 'row', axis=1, tiled=True)  34.4 us
    all_to_all x1, blocking collectives, on_device(): merger_in = lax.all_to_all(merger_chunk, 'col', 0, 1, tiled=True)  14.1 us
  transfers between devices with their start and end apart: 5, of which 4 were waited for; matrix products, arithmetic and copies ran while one was open for 52% of the time, Pallas kernels for 0%

commit v1 on v0

--- a/solution.py
+++ b/solution.py
@@ -28,7 +28,16 @@
     heads_here = local_width // HD
     score_scale = HD ** (-0.5)
     col_index = lax.axis_index("col")
-    full_rows = lax.all_gather(hidden, "col", axis=0, tiled=True)
+    ways = lax.axis_size("col")
+    up = [(d, (d + 1) % ways) for d in range(ways)]
+    down = [(d, (d - 1) % ways) for d in range(ways)]
+    earlier, later = ([hidden], [hidden])
+    for _ in range(ways // 2):
+        earlier.append(lax.ppermute(earlier[-1], "col", up))
+    for _ in range((ways - 1) // 2):
+        later.append(lax.ppermute(later[-1], "col", down))
+    line = jnp.concatenate([*earlier[::-1], *later[1:]], axis=0)
+    full_rows = jnp.roll(line, (lax.axis_index("col") - ways // 2) * hidden.shape[0], axis=0)
     out_weight = lax.all_gather(w_out, "col", axis=0, tiled=True)
     full_float = full_rows.astype(jnp.float32)
     in_mean = jnp.sum(full_float, axis=0, keepdims=True) / model_width

time: 534 us -> 614 us (1.15)
  starting transfers between devices: 7.17 us -> 41.7 us
  local copies, waits for them, and re-layouts: 33.4 us -> 53.4 us
  other arithmetic: 97.5 us -> 111 us
  waiting for transfers between devices: 179 us -> 188 us
    ppermute x0 -> x15, waiting for transfers between devices: none -> 72.7 us  [the longest x8 72.6 us: on_device(): earlier.append(lax.ppermute(earlier[-1], 'col', up))]
    all_gather x1 -> x0, waiting for transfers between devices: 58.2 us -> none  [on_device(): full_rows = lax.all_gather(hidden, 'col', axis=0, tiled=True)]
    ppermute x0 -> x15, starting transfers between devices: none -> 34.5 us  [the longest x7 32.8 us: on_device(): later.append(lax.ppermute(later[-1], 'col', down))]
    concatenate x0 -> x1, local copies, waits for them, and re-layouts: none -> 23.8 us  [on_device(): jnp.roll(line, (lax.axis_index('col') - ways // 2) * hidden.shape[0], axi...]
    all_gather x1 -> x0, local copies, waits for them, and re-layouts: 8.35 us -> none  [on_device(): full_rows = lax.all_gather(hidden, 'col', axis=0, tiled=True)]
  transfers between devices with their start and end apart: 5 -> 19, of which waited for: 4 -> 10; matrix products, arithmetic and copies ran while one was open for 52% -> 46% of each run, Pallas kernels for 0% -> 0%
where the time goes in v1:
time: 614 us; the launch traced here: 610 us
  waiting for transfers between devices  188 us (31%)
  matrix products  186 us (30%)
  other arithmetic  111 us (18%)
  local copies, waits for them, and re-layouts  53.4 us (9%)
  starting transfers between devices  41.7 us (7%)
  blocking collectives  16.5 us (3%)
  between operations  13.4 us (2%)
    dot_general x16, matrix products, take_block(): jnp.einsum('hdq,hdk->hqk', query_heads, key_block, preferred_element_type...  88.8 us
    dot_general x16, matrix products, take_block(): jnp.einsum('hqk,hdk->hdq', weights_exp.astype(jnp.bfloat16), value_block,...  86.5 us
    psum x1, waiting for transfers between devices, on_device(): merged_sum = lax.psum(merged.astype(jnp.bfloat16), 'col')  82.7 us
    reduce_sum x16, other arithmetic, take_block(): running_sum = running_sum * factor + jnp.sum(weights_exp, axis=2)  73.5 us
    ppermute x8, waiting for transfers between devices, on_device(): earlier.append(lax.ppermute(earlier[-1], 'col', up))  72.6 us
    ppermute x7, starting transfers between devices, on_device(): later.append(lax.ppermute(later[-1], 'col', down))  32.8 us
    all_gather x1, waiting for transfers between devices, on_device(): pair_all = lax.all_gather(pair_local, 'row', axis=1, tiled=True)  31.6 us
    concatenate x1, local copies, waits for them, and re-layouts, on_device(): jnp.roll(line, (lax.axis_index('col') - ways // 2) * hidden.shape[0], axi...  23.8 us
  transfers between devices with their start and end apart: 19, of which 10 were waited for; matrix products, arithmetic and copies ran while one was open for 46% of the time, Pallas kernels for 0%

profile of v1, /device:TPU:0, one launch (start us, length us, event | category | flops | bytes accessed | tf_op | source)
XLA Modules:
  0.0 610.0 jit_solution(11606306978956251496)
XLA Ops:
  13.3 11.8 %collective-permute-done = bf16[88,2048]{0,1:T(8,128)(2,1)S(1)} collective-permute-done((bf16[88,2048]{0,1:T(8,128)(2,1)S(1)}, bf16[88,2048]{0,1:T(8,128)(2,1)S(1)}, u32[]{:S(2)}, u32[]{:S(2)}) %collective-permute-start) | collective-permute-done | bytes 360480 | tf_op jit(solution)/shard_map/ppermute | solution.py:36
  30.5 11.0 %collective-permute-done.1 = bf16[88,2048]{0,1:T(8,128)(2,1)S(1)} collective-permute-done((bf16[88,2048]{0,1:T(8,128)(2,1)S(1)}, bf16[88,2048]{0,1:T(8,128)(2,1)S(1)}, u32[]{:S(2)}, u32[]{:S(2)}) %collective-permute-start.1) | collective-permute-done | bytes 360480 | tf_op jit(solution)/shard_map/ppermute | solution.py:36
  46.9 10.1 %collective-permute-done.2 = bf16[88,2048]{0,1:T(8,128)(2,1)S(1)} collective-permute-done((bf16[88,2048]{0,1:T(8,128)(2,1)S(1)}, bf16[88,2048]{0,1:T(8,128)(2,1)S(1)}, u32[]{:S(2)}, u32[]{:S(2)}) %collective-permute-start.2) | collective-permute-done | bytes 360480 | tf_op jit(solution)/shard_map/ppermute | solution.py:36
  62.4 9.1 %collective-permute-done.3 = bf16[88,2048]{0,1:T(8,128)(2,1)S(1)} collective-permute-done((bf16[88,2048]{0,1:T(8,128)(2,1)S(1)}, bf16[88,2048]{0,1:T(8,128)(2,1)S(1)}, u32[]{:S(2)}, u32[]{:S(2)}) %collective-permute-start.3) | collective-permute-done | bytes 360480 | tf_op jit(solution)/shard_map/ppermute | solution.py:36
  77.0 8.2 %collective-permute-done.4 = bf16[88,2048]{0,1:T(8,128)(2,1)S(1)} collective-permute-done((bf16[88,2048]{0,1:T(8,128)(2,1)S(1)}, bf16[88,2048]{0,1:T(8,128)(2,1)S(1)}, u32[]{:S(2)}, u32[]{:S(2)}) %collective-permute-start.4) | collective-permute-done | bytes 360480 | tf_op jit(solution)/shard_map/ppermute | solution.py:36
  90.6 7.3 %collective-permute-done.5 = bf16[88,2048]{0,1:T(8,128)(2,1)S(1)} collective-permute-done((bf16[88,2048]{0,1:T(8,128)(2,1)S(1)}, bf16[88,2048]{0,1:T(8,128)(2,1)S(1)}, u32[]{:S(2)}, u32[]{:S(2)}) %collective-permute-start.5) | collective-permute-done | bytes 360480 | tf_op jit(solution)/shard_map/ppermute | solution.py:36
  103.2 7.5 %collective-permute-done.6 = bf16[88,2048]{0,1:T(8,128)(2,1)} collective-permute-done((bf16[88,2048]{0,1:T(8,128)(2,1)S(1)}, bf16[88,2048]{0,1:T(8,128)(2,1)}, u32[]{:S(2)}, u32[]{:S(2)}) %collective-permute-start.6) | collective-permute-done | bytes 360480 | tf_op jit(solution)/shard_map/ppermute | solution.py:36
  115.9 7.6 %collective-permute-done.7 = bf16[88,2048]{0,1:T(8,128)(2,1)} collective-permute-done((bf16[88,2048]{0,1:T(8,128)(2,1)}, bf16[88,2048]{0,1:T(8,128)(2,1)}, u32[]{:S(2)}, u32[]{:S(2)}) %collective-permute-start.7) | collective-permute-done | bytes 360480 | tf_op jit(solution)/shard_map/ppermute | solution.py:36
  123.5 23.8 %concatenate.9 = bf16[2816,2048]{0,1:T(8,128)(2,1)} concatenate(bf16[88,2048]{0,1:T(8,128)(2,1)} %collective-permute-done.7, bf16[88,2048]{0,1:T(8,128)(2,1)} %collective-permute-done.6, bf16[88,2048]{0,1:T(8,128)(2,1)} %copy-done.10, bf16[88,2048]{0,1:T(8,128)(2,1)} %copy-done.8, bf16[88,2048]{0,1:T(8,128)(2,1)} %copy-done.6, bf16[88,2048]{0,1:T(8,128)(2,1)} %copy-done.4, ...), dimensions={0} | concatenate | bytes 23068672 | tf_op jit(solution)/shard_map/jit(_roll_dynamic)/concatenate | solution.py:40
  147.3 10.0 %convert_reduce_fusion = (f32[2048]{0:T(1024)S(1)}, f32[2048]{0:T(1024)S(1)}) fusion(bf16[2816,2048]{0,1:T(8,128)(2,1)} %concatenate.9, s32[]{:T(128)S(6)} %select_n.100), kind=kLoop, calls=%fused_computation.30 | loop fusion | flops 11530240 | bytes 5783556 | tf_op jit(solution)/shard_map/reduce_sum | solution.py:43
  157.4 9.4 %multiply_convert_fusion = bf16[1408,2048]{0,1:T(8,128)(2,1)} fusion(f32[1408]{0:T(1024)S(1)} %convert_element_type.51, f32[2048]{0:T(1024)S(1)} %get-tuple-element.200, f32[2048]{0:T(1024)S(1)} %get-tuple-element.199, bf16[2816,2048]{0,1:T(8,128)(2,1)} %concatenate.9, s32[]{:T(128)S(6)} %select_n.100), kind=kLoop, calls=%fused_computation.28 | loop fusion | flops 14417920 | bytes 11556356 | tf_op jit(solution)/shard_map/convert_element_type | solution.py:49
  172.4 6.9 %scatter_fusion = bf16[2,88,2048]{1,0,2:T(2,128)(2,1)S(1)} fusion(bf16[2,88,2048]{1,0,2:T(2,128)(2,1)S(1)} %copy.45, s32[200]{0:T(256)S(1)} %bitcast.123, bf16[200,2,88]{2,1,0:T(2,128)(2,1)S(1)} %bitcast.116), kind=kCustom, calls=%fused_computation.2 | custom fusion | bytes 212000 | tf_op jit(solution)/shard_map/scatter | solution.py:59
  186.5 31.6 %all-gather.3.cloned.1.call-done = bf16[177,16384]{1,0:T(8,128)(2,1)} async-done(((bf16[177,2048]{1,0:T(8,128)(2,1)}), bf16[177,16384]{1,0:T(8,128)(2,1)}) %all-gather.3.cloned.1.call-update) | async-done | bytes 5799952 | tf_op jit(solution)/shard_map/all_gather | solution.py:65
  218.1 5.7 slice.29
  224.8 250.7 %while.18 = (s32[]{:T(128)}, f32[1,2048]{1,0:T(1,128)S(1)}, f32[1,2048]{1,0:T(1,128)S(1)}, f32[1,88,2048]{2,1,0:T(8,128)S(1)}, s32[2048]{0:T(1024)S(1)}, /*index...) while((s32[]{:T(128)}, f32[1,2048]{1,0:T(1,128)S(1)}, ...), condition=%wide.region_6.7_spmd.clone, body=%wide.region_3.6_spmd.clone.sunk | while | flops 768108544 | bytes 27504848 | solution.py:106
  240.6 5.6 fusion.44
  256.3 5.6 fusion.44
  272.1 5.5 fusion.44
  287.8 5.5 fusion.44
  303.4 5.5 fusion.44
  319.1 5.5 fusion.44
  334.7 5.5 fusion.44
  350.4 5.5 fusion.44
  366.0 5.5 fusion.44
  381.7 5.5 fusion.44
  397.3 5.5 fusion.44
  413.0 5.5 fusion.44
  428.6 5.5 fusion.44
  476.5 6.9 %all-to-all-start = ((bf16[88,16,128]{2,0,1:T(8,128)(2,1)}), bf16[88,16,128]{2,0,1:T(8,128)(2,1)S(1)}, u32[]{:S(2)}, u32[]{:S(2)}) async-start(bf16[88,16,128]{2,0,1:T(8,128)(2,1)} %copy.47), calls=%async_computation | async-start | bytes 720896 | tf_op jit(solution)/shard_map/all_to_all | solution.py:111
  483.7 9.8 %dynamic-slice_convert_fusion = f32[1408,2048]{0,1:T(8,128)} fusion(bf16[2816,2048]{0,1:T(8,128)(2,1)} %concatenate.9, s32[]{:T(128)S(6)} %select_n.100), kind=kLoop, calls=%fused_computation.31 | loop fusion | flops 2883584 | bytes 17301508 | tf_op jit(solution)/shard_map/convert_element_type | solution.py:42
  497.1 16.5 %all_to_all.35 = bf16[16,88,128]{2,1,0:T(8,128)(2,1)S(1)} all-to-all(bf16[16,88,128]{2,1,0:T(8,128)(2,1)S(1)} %bitcast.112), channel_id=1, replica_groups=mesh['row'=8,'col'=16] {'col'}, dimensions={0} | all-to-all | bytes 720896 | tf_op jit(solution)/shard_map/all_to_all | solution.py:124
  517.5 82.7 %all-reduce.2.cloned.1.call-done = bf16[512,1408]{1,0:T(8,128)(2,1)} async-done(((bf16[512,1408]{1,0:T(8,128)(2,1)}), bf16[512,1408]{1,0:T(8,128)(2,1)}) %all-reduce.2.cloned.1.call-update) | async-done | bytes 1441808 | tf_op jit(solution)/shard_map/psum | solution.py:128
  (193 shorter events, 247.6 us)
Async XLA Ops:
  6.5 507.4 %copy-start = (bf16[4,88,1408]{2,1,0:T(8,128)(2,1)S(1)}, bf16[4,88,1408]{2,1,0:T(8,128)(2,1)}, u32[]{:S(2)}) copy-start(bf16[4,88,1408]{2,1,0:T(8,128)(2,1)} %param.22) | copy-start | bytes 2973700
  6.5 211.6 %all-gather.3.cloned.1.call-start = ((), (), s32[]{:S(2)}) async-start(), calls=%async_computation.2 | async-start | bytes 6782976 | tf_op jit(solution)/shard_map/all_gather | solution.py:65
  7.9 17.3 %collective-permute-start = (bf16[88,2048]{0,1:T(8,128)(2,1)S(1)}, bf16[88,2048]{0,1:T(8,128)(2,1)S(1)}, u32[]{:S(2)}, u32[]{:S(2)}) collective-permute-start(bf16[88,2048]{0,1:T(8,128)(2,1)S(1)} %copy.40), channel_id=1, source_target_pairs={{0,1},{1,2},{2,3},{3,4},{4,5},{5,6},{6,7},{7,8},{8,9},{9,10},{10,1... | collective-permute-start | bytes 1081352 | tf_op jit(solution)/shard_map/ppermute | solution.py:36
  9.5 15.6 %collective-permute-start.8 = (bf16[88,2048]{0,1:T(8,128)(2,1)S(1)}, bf16[88,2048]{0,1:T(8,128)(2,1)S(1)}, u32[]{:S(2)}, u32[]{:S(2)}) collective-permute-start(bf16[88,2048]{0,1:T(8,128)(2,1)S(1)} %copy.40), channel_id=1, source_target_pairs={{0,15},{1,0},{2,1},{3,2},{4,3},{5,4},{6,5},{7,6},{8,7},{9,8},{10,9... | collective-permute-start | bytes 1081352 | tf_op jit(solution)/shard_map/ppermute | solution.py:38
  25.2 16.4 %collective-permute-start.1 = (bf16[88,2048]{0,1:T(8,128)(2,1)S(1)}, bf16[88,2048]{0,1:T(8,128)(2,1)S(1)}, u32[]{:S(2)}, u32[]{:S(2)}) collective-permute-start(bf16[88,2048]{0,1:T(8,128)(2,1)S(1)} %collective-permute-done), channel_id=1, source_target_pairs={{0,1},{1,2},{2,3},{3,4},{4,5},{5,6},{6,7},{7,8},{8,9},{9,10},{10,1... | collective-permute-start | bytes 1081352 | tf_op jit(solution)/shard_map/ppermute | solution.py:36
  25.2 86.2 %copy-start.1 = (bf16[88,2048]{0,1:T(8,128)(2,1)}, bf16[88,2048]{0,1:T(8,128)(2,1)S(1)}, u32[]{:S(2)}) copy-start(bf16[88,2048]{0,1:T(8,128)(2,1)S(1)} %collective-permute-done.8) | copy-start | bytes 1081348
  25.2 16.4 %collective-permute-start.9 = (bf16[88,2048]{0,1:T(8,128)(2,1)S(1)}, bf16[88,2048]{0,1:T(8,128)(2,1)S(1)}, u32[]{:S(2)}, u32[]{:S(2)}) collective-permute-start(bf16[88,2048]{0,1:T(8,128)(2,1)S(1)} %collective-permute-done.8), channel_id=1, source_target_pairs={{0,15},{1,0},{2,1},{3,2},{4,3},{5,4},{6,5},{7,6},{8,7},{9,8},{10,9... | collective-permute-start | bytes 1081352 | tf_op jit(solution)/shard_map/ppermute | solution.py:38
  41.5 69.8 %copy-start.2 = (bf16[88,2048]{0,1:T(8,128)(2,1)}, bf16[88,2048]{0,1:T(8,128)(2,1)S(1)}, u32[]{:S(2)}) copy-start(bf16[88,2048]{0,1:T(8,128)(2,1)S(1)} %collective-permute-done.1) | copy-start | bytes 1081348
  41.5 15.5 %collective-permute-start.2 = (bf16[88,2048]{0,1:T(8,128)(2,1)S(1)}, bf16[88,2048]{0,1:T(8,128)(2,1)S(1)}, u32[]{:S(2)}, u32[]{:S(2)}) collective-permute-start(bf16[88,2048]{0,1:T(8,128)(2,1)S(1)} %collective-permute-done.1), channel_id=1, source_target_pairs={{0,1},{1,2},{2,3},{3,4},{4,5},{5,6},{6,7},{7,8},{8,9},{9,10},{10,1... | collective-permute-start | bytes 1081352 | tf_op jit(solution)/shard_map/ppermute | solution.py:36
  41.6 15.4 %copy-start.3 = (bf16[88,2048]{0,1:T(8,128)(2,1)}, bf16[88,2048]{0,1:T(8,128)(2,1)S(1)}, u32[]{:S(2)}) copy-start(bf16[88,2048]{0,1:T(8,128)(2,1)S(1)} %collective-permute-done.9) | copy-start | bytes 1081348
  41.6 15.4 %collective-permute-start.10 = (bf16[88,2048]{0,1:T(8,128)(2,1)S(1)}, bf16[88,2048]{0,1:T(8,128)(2,1)S(1)}, u32[]{:S(2)}, u32[]{:S(2)}) collective-permute-start(bf16[88,2048]{0,1:T(8,128)(2,1)S(1)} %collective-permute-done.9), channel_id=1, source_target_pairs={{0,15},{1,0},{2,1},{3,2},{4,3},{5,4},{6,5},{7,6},{8,7},{9,8},{10,9... | collective-permute-start | bytes 1081352 | tf_op jit(solution)/shard_map/ppermute | solution.py:38
  57.0 0.8 copy-start.4
  57.0 14.5 %collective-permute-start.3 = (bf16[88,2048]{0,1:T(8,128)(2,1)S(1)}, bf16[88,2048]{0,1:T(8,128)(2,1)S(1)}, u32[]{:S(2)}, u32[]{:S(2)}) collective-permute-start(bf16[88,2048]{0,1:T(8,128)(2,1)S(1)} %collective-permute-done.2), channel_id=1, source_target_pairs={{0,1},{1,2},{2,3},{3,4},{4,5},{5,6},{6,7},{7,8},{8,9},{9,10},{10,1... | collective-permute-start | bytes 1081352 | tf_op jit(solution)/shard_map/ppermute | solution.py:36
  57.8 13.7 %copy-start.5 = (bf16[88,2048]{0,1:T(8,128)(2,1)}, bf16[88,2048]{0,1:T(8,128)(2,1)S(1)}, u32[]{:S(2)}) copy-start(bf16[88,2048]{0,1:T(8,128)(2,1)S(1)} %collective-permute-done.10) | copy-start | bytes 1081348
  57.8 13.7 %collective-permute-start.11 = (bf16[88,2048]{0,1:T(8,128)(2,1)S(1)}, bf16[88,2048]{0,1:T(8,128)(2,1)S(1)}, u32[]{:S(2)}, u32[]{:S(2)}) collective-permute-start(bf16[88,2048]{0,1:T(8,128)(2,1)S(1)} %collective-permute-done.10), channel_id=1, source_target_pairs={{0,15},{1,0},{2,1},{3,2},{4,3},{5,4},{6,5},{7,6},{8,7},{9,8},{10,9... | collective-permute-start | bytes 1081352 | tf_op jit(solution)/shard_map/ppermute | solution.py:38
  71.5 13.6 %collective-permute-start.4 = (bf16[88,2048]{0,1:T(8,128)(2,1)S(1)}, bf16[88,2048]{0,1:T(8,128)(2,1)S(1)}, u32[]{:S(2)}, u32[]{:S(2)}) collective-permute-start(bf16[88,2048]{0,1:T(8,128)(2,1)S(1)} %collective-permute-done.3), channel_id=1, source_target_pairs={{0,1},{1,2},{2,3},{3,4},{4,5},{5,6},{6,7},{7,8},{8,9},{9,10},{10,1... | collective-permute-start | bytes 1081352 | tf_op jit(solution)/shard_map/ppermute | solution.py:36
  72.3 12.8 %copy-start.7 = (bf16[88,2048]{0,1:T(8,128)(2,1)}, bf16[88,2048]{0,1:T(8,128)(2,1)S(1)}, u32[]{:S(2)}) copy-start(bf16[88,2048]{0,1:T(8,128)(2,1)S(1)} %collective-permute-done.11) | copy-start | bytes 1081348
  72.3 12.8 %collective-permute-start.12 = (bf16[88,2048]{0,1:T(8,128)(2,1)S(1)}, bf16[88,2048]{0,1:T(8,128)(2,1)S(1)}, u32[]{:S(2)}, u32[]{:S(2)}) collective-permute-start(bf16[88,2048]{0,1:T(8,128)(2,1)S(1)} %collective-permute-done.11), channel_id=1, source_target_pairs={{0,15},{1,0},{2,1},{3,2},{4,3},{5,4},{6,5},{7,6},{8,7},{9,8},{10,9... | collective-permute-start | bytes 1081352 | tf_op jit(solution)/shard_map/ppermute | solution.py:38
  85.2 12.7 %collective-permute-start.5 = (bf16[88,2048]{0,1:T(8,128)(2,1)S(1)}, bf16[88,2048]{0,1:T(8,128)(2,1)S(1)}, u32[]{:S(2)}, u32[]{:S(2)}) collective-permute-start(bf16[88,2048]{0,1:T(8,128)(2,1)S(1)} %collective-permute-done.4), channel_id=1, source_target_pairs={{0,1},{1,2},{2,3},{3,4},{4,5},{5,6},{6,7},{7,8},{8,9},{9,10},{10,1... | collective-permute-start | bytes 1081352 | tf_op jit(solution)/shard_map/ppermute | solution.py:36
  86.0 11.9 %copy-start.9 = (bf16[88,2048]{0,1:T(8,128)(2,1)}, bf16[88,2048]{0,1:T(8,128)(2,1)S(1)}, u32[]{:S(2)}) copy-start(bf16[88,2048]{0,1:T(8,128)(2,1)S(1)} %collective-permute-done.12) | copy-start | bytes 1081348
  86.0 11.9 %collective-permute-start.13 = (bf16[88,2048]{0,1:T(8,128)(2,1)S(1)}, bf16[88,2048]{0,1:T(8,128)(2,1)}, u32[]{:S(2)}, u32[]{:S(2)}) collective-permute-start(bf16[88,2048]{0,1:T(8,128)(2,1)S(1)} %collective-permute-done.12), channel_id=1, source_target_pairs={{0,15},{1,0},{2,1},{3,2},{4,3},{5,4},{6,5},{7,6},{8,7},{9,8},{10,9... | collective-permute-start | bytes 1081352 | tf_op jit(solution)/shard_map/ppermute | solution.py:38
  97.9 0.9 copy-start.10
  97.9 12.8 %collective-permute-start.6 = (bf16[88,2048]{0,1:T(8,128)(2,1)S(1)}, bf16[88,2048]{0,1:T(8,128)(2,1)}, u32[]{:S(2)}, u32[]{:S(2)}) collective-permute-start(bf16[88,2048]{0,1:T(8,128)(2,1)S(1)} %collective-permute-done.5), channel_id=1, source_target_pairs={{0,1},{1,2},{2,3},{3,4},{4,5},{5,6},{6,7},{7,8},{8,9},{9,10},{10,1... | collective-permute-start | bytes 1081352 | tf_op jit(solution)/shard_map/ppermute | solution.py:36
  98.7 17.2 %collective-permute-start.14 = (bf16[88,2048]{0,1:T(8,128)(2,1)}, bf16[88,2048]{0,1:T(8,128)(2,1)}, u32[]{:S(2)}, u32[]{:S(2)}) collective-permute-start(bf16[88,2048]{0,1:T(8,128)(2,1)} %collective-permute-done.13), channel_id=1, source_target_pairs={{0,15},{1,0},{2,1},{3,2},{4,3},{5,4},{6,5},{7,6},{8,7},{9,8},{10,9... | collective-permute-start | bytes 1081352 | tf_op jit(solution)/shard_map/ppermute | solution.py:38
  110.7 12.8 %collective-permute-start.7 = (bf16[88,2048]{0,1:T(8,128)(2,1)}, bf16[88,2048]{0,1:T(8,128)(2,1)}, u32[]{:S(2)}, u32[]{:S(2)}) collective-permute-start(bf16[88,2048]{0,1:T(8,128)(2,1)} %collective-permute-done.6), channel_id=1, source_target_pairs={{0,1},{1,2},{2,3},{3,4},{4,5},{5,6},{6,7},{7,8},{8,9},{9,10},{10,1... | collective-permute-start | bytes 1081352 | tf_op jit(solution)/shard_map/ppermute | solution.py:36
  157.4 14.4 %copy-start.14 = (bf16[2,88,1408]{2,1,0:T(8,128)(2,1)S(1)}, bf16[2,88,1408]{2,1,0:T(8,128)(2,1)}, u32[]{:S(2)}) copy-start(bf16[2,88,1408]{2,1,0:T(8,128)(2,1)} %param.16) | copy-start | bytes 1486852
  166.8 15.0 %copy-start.13 = (bf16[1408]{0:T(1024)(128)(2,1)S(1)}, bf16[1408]{0:T(1024)(128)(2,1)}, u32[]{:S(2)}) copy-start(bf16[1408]{0:T(1024)(128)(2,1)} %param.21) | copy-start | bytes 8452
  166.8 15.0 %copy-start.12 = (bf16[88,1408]{1,0:T(8,128)(2,1)S(1)}, bf16[88,1408]{1,0:T(8,128)(2,1)}, u32[]{:S(2)}) copy-start(bf16[88,1408]{1,0:T(8,128)(2,1)} %param.15) | copy-start | bytes 743428
  181.0 312.4 %all-gather.5.cloned.1.call-start = ((), (), s32[]{:S(2)}) async-start(), calls=%async_computation.3 | async-start | bytes 4212736 | tf_op jit(solution)/shard_map/all_gather | solution.py:41
  181.8 43.0 %copy-start.11 = (s32[2048]{0:T(1024)S(1)}, s32[2048]{0:T(1024)}, u32[]{:S(2)}) copy-start(s32[2048]{0:T(1024)} %param.19) | copy-start | bytes 24580
  476.5 17.0 %all-to-all-start = ((bf16[88,16,128]{2,0,1:T(8,128)(2,1)}), bf16[88,16,128]{2,0,1:T(8,128)(2,1)S(1)}, u32[]{:S(2)}, u32[]{:S(2)}) async-start(bf16[88,16,128]{2,0,1:T(8,128)(2,1)} %copy.47), calls=%async_computation | async-start | bytes 720896 | tf_op jit(solution)/shard_map/all_to_all | solution.py:111
  483.4 116.8 %all-reduce.2.cloned.1.call-start = ((), (), s32[]{:S(2)}) async-start(), calls=%async_computation.4 | async-start | bytes 2883584 | tf_op jit(solution)/shard_map/psum | solution.py:128
  (2 other events, 1.6 us)
Sparse Core Ops, SparseCore 0:
  181.1 36.9 all-gather.2
  220.2 50.4 all-gather.4
  516.2 83.9 all-reduce.1
